TPU v7x, 256 devices: a whole 4x4x8 slice. The times are simulated.
256 devices in a mesh: seq: 64 (over y, z, x_hi), tp: 4 (over x_lo, core).
Axes of the slice: x: 4 (x_hi: 2, x_lo: 2; x = x_hi * 2 + x_lo), y: 4, z: 8, core: 2. Of those that a mesh axis runs over, the one named last changes fastest.
Arguments:
- query_input: bfloat16 [8192, 4096], P('seq', 'tp'), may hold values from -6 to 6
- key_input: bfloat16 [8192, 4096], P('seq', 'tp'), may hold values from -6 to 6
- value_input: bfloat16 [8192, 4096], P('seq', 'tp'), may hold values from -6 to 6
- short_filter: float32 [3, 3, 4096], P(None, None, 'tp'), may hold values from -3 to 3
- residues: float32 [16, 4096], P(None, 'tp'), may hold values from -1.5 to 1.5
- decays: float32 [16, 4096], P(None, 'tp'), as said below
- skip_gain: float32 [4096], P('tp'), may hold values from -4 to 4
- head_weight: bfloat16 [32, 4096, 128], P(None, ('tp', 'seq')), may hold values from -0.015625 to 0.015625
Outputs:
- operator_out: bfloat16 [8192, 4096], P('seq', 'tp')
- probe_out: bfloat16 [512, 128], P(('seq', 'tp'))
Inputs may be any that keep to these rules, and one draw needn't show every extreme that they name: `decays`: each rate is positive, at least 1 / 16384 and at most 1 / 30.
All inputs are finite; a program needn't handle non-finite values.
Results may differ from a plain program's by a relative error of at most 0.01.
Values may be sent and summed in bfloat16 or wider, within the bound.
No kernel may reach another device: no remote copies, remote signals or barrier semaphores. Data moves between devices by JAX's collectives and lax.ppermute only.
A program may use at most 64 MiB of HBM per device.

v0:
```python
import jax
import jax.numpy as jnp
from jax import lax
from jax.sharding import PartitionSpec as P

STRIDE = 16
CHUNK = 128
highest = lax.Precision.HIGHEST


def from_behind(block, axis, distance):
    devices = range(lax.axis_size(axis))
    route = [(i - distance, i) for i in devices if i - distance in devices]
    return lax.ppermute(block, axis, route)


def short_pass(rows, before, tap_weights):
    joined = jnp.concatenate([before, rows], axis=0).astype(jnp.float32)
    row_count = rows.shape[0]
    return (
        tap_weights[0] * joined[2 : 2 + row_count]
        + tap_weights[1] * joined[1 : 1 + row_count]
        + tap_weights[2] * joined[0:row_count]
    )


def modal_conv(gated, residues, decays):
    span, width = gated.shape
    chunks = span // CHUNK
    groups = lax.axis_size("u")
    g = gated.astype(jnp.float32).reshape(chunks, CHUNK, width)
    steps = jnp.arange(CHUNK, dtype=jnp.float32)
    weight = residues * jnp.sqrt(-jnp.expm1(-2.0 * decays))
    grow = jnp.exp(decays[:, None, :] * steps[None, :, None])
    shrink = jnp.exp(-decays[:, None, :] * steps[None, :, None])
    lower = (steps[:, None] >= steps[None, :]).astype(jnp.float32)
    running = jnp.einsum("ij,rkjc->rkic", lower, grow[:, None] * g[None], precision=highest)
    ends = jnp.exp(-decays * (CHUNK - 1))[:, None, :] * running[:, :, -1, :]
    index = jnp.arange(chunks)
    lag = (index[:, None] - 1 - index[None, :]).astype(jnp.float32)
    decay_table = jnp.where(
        (lag >= 0)[None, :, :, None],
        jnp.exp(-decays[:, None, None, :] * (CHUNK * jnp.maximum(lag, 0.0))[None, :, :, None]),
        0.0,
    )
    inner = jnp.sum(decay_table * ends[:, None, :, :], axis=2)
    total = jnp.exp(-decays * CHUNK) * inner[:, -1] + ends[:, -1]
    outer = None
    for m in range(1, groups):
        term = from_behind(total, "u", m)
        if m > 1:
            term = jnp.exp(-decays * float(span * (m - 1))) * term
        outer = term if outer is None else outer + term
    if outer is not None:
        offsets = (CHUNK * index).astype(jnp.float32)
        inner = inner + jnp.exp(-decays[:, None, :] * offsets[None, :, None]) * outer[:, None, :]
    after = jnp.exp(-decays[:, None, :] * (steps[None, :, None] + 1.0))
    modes = shrink[:, None] * running + after[:, None] * inner[:, :, None, :]
    return jnp.sum(weight[:, None, None, :] * modes, axis=0).reshape(span, width)


def shards(
    query_input, key_input, value_input, short_filter, residues, decays, skip_gain, head_weight
):
    tokens, chan_width = query_input.shape
    width_u = lax.axis_size("u")
    width_v = lax.axis_size("v")
    piece = head_weight.shape[1]
    span = tokens * width_v
    narrow = width_u * piece
    stacked = jnp.stack([query_input, key_input, value_input], axis=0)
    stacked = stacked.reshape(1, 3, tokens, width_u, width_v, piece)
    columns = lax.all_to_all(stacked, "v", split_axis=4, concat_axis=0, tiled=True)
    columns = columns.reshape(width_v, 3, tokens, narrow)
    columns = jnp.transpose(columns, (1, 0, 2, 3)).reshape(3, span, narrow)
    weight_rep = jnp.broadcast_to(head_weight[None], (width_u,) + head_weight.shape)
    weight_cols = lax.all_to_all(weight_rep, "u", split_axis=0, concat_axis=0, tiled=True)
    weight_cols = jnp.transpose(weight_cols, (1, 0, 2, 3)).reshape(
        head_weight.shape[0], narrow, head_weight.shape[2]
    )
    before = from_behind(columns[:, -2:], "u", 1)
    sf = short_filter.reshape(3, 3, width_u, width_v, piece)
    sf = jnp.transpose(sf, (0, 1, 3, 2, 4))
    sf = lax.dynamic_index_in_dim(sf, lax.axis_index("v"), axis=2, keepdims=False)
    sf = sf.reshape(3, 3, narrow)

    def pick(values):
        shaped = values.reshape(values.shape[0], width_u, width_v, piece)
        shaped = lax.dynamic_index_in_dim(shaped, lax.axis_index("v"), axis=2, keepdims=False)
        return shaped.reshape(values.shape[0], narrow)

    query_short = short_pass(columns[0], before[0], sf[:, 0])
    key_short = short_pass(columns[1], before[1], sf[:, 1])
    value_short = short_pass(columns[2], before[2], sf[:, 2])
    gated = (key_short * value_short).astype(jnp.bfloat16)
    convolved = modal_conv(gated, pick(residues), pick(decays))
    gain = pick(skip_gain[None])[0]
    carried = (convolved + gain * gated.astype(jnp.float32)).astype(jnp.bfloat16)
    op_cols = (query_short * carried.astype(jnp.float32)).astype(jnp.bfloat16)
    back = op_cols.reshape(width_v, tokens, width_u, 1, piece)
    back = lax.all_to_all(back, "v", split_axis=0, concat_axis=3, tiled=True)
    operator_out = back.reshape(tokens, chan_width)
    rim_rows = from_behind(op_cols[:STRIDE], "u", -1)
    extended = jnp.concatenate([op_cols, rim_rows], axis=0)
    rows = span // STRIDE
    early_rows = extended[:span].reshape(rows, STRIDE, narrow)
    late_rows = extended[STRIDE:].reshape(rows, STRIDE, narrow)
    running = jnp.einsum(
        "jic,ico->jo", early_rows, weight_cols[:STRIDE], preferred_element_type=jnp.float32
    )
    partial_sum = running + jnp.einsum(
        "jic,ico->jo", late_rows, weight_cols[STRIDE:], preferred_element_type=jnp.float32
    )
    partial_sum = partial_sum.reshape(width_v, rows // width_v, -1)
    partial_sum = lax.all_to_all(partial_sum, "v", split_axis=0, concat_axis=0, tiled=True)
    block_sum = jnp.sum(partial_sum, axis=0)
    probe_out = lax.psum_scatter(block_sum, "tp", scatter_dimension=0, tiled=True).astype(
        jnp.bfloat16
    )
    return (operator_out, probe_out)


def solution(mesh):
    seq_size, tp_size = mesh.devices.shape
    width_u = 4 if seq_size % 4 == 0 else 1
    split = jax.sharding.Mesh(
        mesh.devices.reshape(width_u, seq_size // width_u, tp_size), ("u", "v", "tp")
    )
    seq = ("u", "v")
    placed = (
        P(seq, "tp"),
        P(seq, "tp"),
        P(seq, "tp"),
        P(None, None, "tp"),
        P(None, "tp"),
        P(None, "tp"),
        P("tp"),
        P(None, ("tp", "u", "v"), None),
    )
    return jax.shard_map(
        shards,
        mesh=split,
        in_specs=placed,
        out_specs=(P(seq, "tp"), P(("u", "v", "tp"), None)),
        check_vma=False,
    )
```

profile of v0, /device:TPU:16, one launch (start us, length us, event | category | flops | bytes accessed | tf_op | source)
XLA Modules:
  0.0 130.6 jit_solution(3539531333170131644)
XLA Ops:
  0.6 1.2 copy.108
  1.8 1.1 copy.107
  2.9 1.1 copy.106
  4.1 0.1 pad_maximum_fusion
  4.2 1.1 copy.109
  5.3 11.0 %all-to-all-start = ((bf16[1,3,128,4,16,16]{2,5,3,1,0,4:T(8,128)(2,1)}), bf16[1,3,128,4,16,16]{2,5,3,1,0,4:T(8,128)(2,1)S(1)}, u32[]{:S(2)}, u32[]{:S(2)}) async-start(bf16[1,3,128,4,16,16]{2,5,3,1,0,4:T(8,128)(2,1)} %copy.109), calls=%async_computation | async-start | bytes 1572864 | tf_op jit(solution)/shard_map/all_to_all | solution.py:73
  16.3 0.9 reshape.209
  17.3 0.1 dynamic-slice_reduce_fusion
  17.4 0.1 reshape.210
  17.4 1.0 reshape.215
  18.5 1.0 reshape.213
  19.6 0.1 reshape.216
  19.7 0.1 reshape.214
  19.8 0.1 convert_compare_fusion
  19.9 0.1 maximum_multiply_fusion
  20.0 0.2 multiply_exponential_fusion.1
  20.2 0.2 multiply_exponential_fusion.2
  20.4 20.5 %all-to-all-done = bf16[1,3,128,4,16,16]{2,5,3,1,0,4:T(8,128)(2,1)S(1)} async-done(((bf16[1,3,128,4,16,16]{2,5,3,1,0,4:T(8,128)(2,1)}), bf16[1,3,128,4,16,16]{2,5,3,1,0,4:T(8,128)(2,1)S(1)}, u32[]{:S(2)}, u32[]{:S(2)}) %all-to-all-start) | async-done | bytes 786464 | tf_op jit(solution)/shard_map/all_to_all | solution.py:73
  40.9 0.9 broadcast_in_dim.12
  41.8 4.8 %all-to-all-start.2 = ((bf16[4,32,16,128]{3,2,1,0:T(8,128)(2,1)}), bf16[4,32,16,128]{3,2,1,0:T(8,128)(2,1)S(1)}, u32[]{:S(2)}, u32[]{:S(2)}) async-start(bf16[4,32,16,128]{3,2,1,0:T(8,128)(2,1)} %broadcast_in_dim.12), calls=%async_computation.2 | async-start | bytes 1048576 | tf_op jit(solution)/shard_map/all_to_all | solution.py:77
  46.6 0.2 copy.161
  46.8 0.1 slice.161
  46.9 3.3 %collective-permute-start = (bf16[3,2,64]{1,2,0:T(8,128)(2,1)S(1)}, bf16[3,2,64]{1,2,0:T(8,128)(2,1)S(1)}, u32[]{:S(2)}, u32[]{:S(2)}) collective-permute-start(bf16[3,2,64]{1,2,0:T(8,128)(2,1)S(1)} %slice.161), channel_id=1, source_target_pairs={{0,64},{64,128},{128,192},{1,65},{65,129},{129,193},{2,66},{66,130... | collective-permute-start | bytes 2312 | tf_op jit(solution)/shard_map/ppermute | solution.py:14
  50.2 0.2 copy.112
  50.4 0.1 copy.165
  50.5 0.2 copy.117
  50.7 0.1 copy.164
  50.7 0.2 copy.120
  50.9 0.1 copy.163
  51.0 1.9 %collective-permute-done = bf16[3,2,64]{1,2,0:T(8,128)(2,1)S(1)} collective-permute-done((bf16[3,2,64]{1,2,0:T(8,128)(2,1)S(1)}, bf16[3,2,64]{1,2,0:T(8,128)(2,1)S(1)}, u32[]{:S(2)}, u32[]{:S(2)}) %collective-permute-start) | collective-permute-done | bytes 800 | tf_op jit(solution)/shard_map/ppermute | solution.py:14
  52.9 0.1 maximum_convert_fusion.2
  53.0 0.3 maximum_convert_fusion
  53.3 0.7 convert_bitcast_fusion
  54.0 4.2 %fusion.4 = f32[16,16,128,64]{2,3,1,0:T(8,128)S(1)} fusion(f32[16,128,64]{1,2,0:T(8,128)S(1)} %bitcast.121, f32[16,128,64]{1,2,0:T(8,128)S(1)} %multiply_exponential_fusion.1), kind=kOutput, calls=%fused_computation.5 | convolution fusion | flops 3223339008 | bytes 9437184 | tf_op jit(solution)/shard_map/ij,rkjc->rkic/dot_general | solution.py:37
  58.3 3.2 %copy-done = f32[16,16,128,64]{2,3,1,0:T(8,128)} copy-done((f32[16,16,128,64]{2,3,1,0:T(8,128)}, f32[16,16,128,64]{2,3,1,0:T(8,128)S(1)}, u32[]{:S(2)}) %copy-start) | copy-done | bytes 8388632
  61.5 5.5 %slice.185 = f32[16,16,1,64]{2,3,1,0:T(8,128)} slice(f32[16,16,128,64]{2,3,1,0:T(8,128)S(1)} %fusion.4), slice={[0:16], [0:16], [127:128], [0:64]} | slice | bytes 131072 | tf_op jit(solution)/shard_map/slice | solution.py:38
  67.0 5.4 %copy.139 = f32[16,16,1,64]{3,0,1,2:T(8,128)S(1)} copy(f32[16,16,1,64]{2,3,1,0:T(8,128)} %slice.185) | data formatting | bytes 131072 | tf_op jit(solution)/shard_map/squeeze | solution.py:38
  72.5 1.3 multiply_reduce_fusion.1
  73.8 0.7 collective-permute-start.3
  74.4 3.7 %collective-permute-start.1 = (f32[16,64]{1,0:T(8,128)S(1)}, f32[16,64]{1,0:T(8,128)S(1)}, u32[]{:S(2)}, u32[]{:S(2)}) collective-permute-start(f32[16,64]{1,0:T(8,128)S(1)} %fusion.25), channel_id=1, source_target_pairs={{0,64},{64,128},{128,192},{1,65},{65,129},{129,193},{2,66},{66,130... | collective-permute-start | bytes 12296 | tf_op jit(solution)/shard_map/ppermute | solution.py:14
  78.2 1.3 collective-permute-start.2
  79.5 0.1 reshape_broadcast_in_dim.3
  79.6 0.1 mul.408
  79.7 0.3 collective-permute-done.1
  80.0 5.2 %collective-permute-done.2 = f32[16,64]{1,0:T(8,128)S(1)} collective-permute-done((f32[16,64]{1,0:T(8,128)S(1)}, f32[16,64]{1,0:T(8,128)S(1)}, u32[]{:S(2)}, u32[]{:S(2)}) %collective-permute-start.2) | collective-permute-done | bytes 4128 | tf_op jit(solution)/shard_map/ppermute | solution.py:14
  85.2 0.1 multiply_add_fusion
  85.3 5.4 %multiply_reduce_fusion = f32[16,128,64]{1,2,0:T(8,128)S(1)} fusion(f32[16,16,128,64]{2,3,1,0:T(8,128)} %copy-done, f32[16,16,64]{2,1,0:T(8,128)S(1)} %multiply_add_fusion, f32[16,128,64]{1,2,0:T(8,128)S(1)} %get-tuple-element.26, f32[16,128,64]{1,2,0:T(8,128)S(1)} %get-tuple-element.25, f32[16,64]{1,0:T(8,128)S(1)} %get-tuple-element.22), kind=kLoop, calls=%fused_computation | loop fusion | flops 10354688 | bytes 10031104 | tf_op jit(solution)/shard_map/reduce_sum | solution.py:59
  90.7 0.4 fusion.19
  91.2 1.9 %collective-permute-start.4 = (bf16[16,64]{0,1:T(8,128)(2,1)S(1)}, bf16[16,64]{0,1:T(8,128)(2,1)S(1)}, u32[]{:S(2)}, u32[]{:S(2)}) collective-permute-start(bf16[16,64]{0,1:T(8,128)(2,1)S(1)} %slice.189), channel_id=1, source_target_pairs={{64,0},{128,64},{192,128},{65,1},{129,65},{193,129},{66,2},{130,66... | collective-permute-start | bytes 6152 | tf_op jit(solution)/shard_map/ppermute | solution.py:14
  93.2 0.3 copy.128
  93.5 3.3 %collective-permute-done.4 = bf16[16,64]{0,1:T(8,128)(2,1)S(1)} collective-permute-done((bf16[16,64]{0,1:T(8,128)(2,1)S(1)}, bf16[16,64]{0,1:T(8,128)(2,1)S(1)}, u32[]{:S(2)}, u32[]{:S(2)}) %collective-permute-start.4) | collective-permute-done | bytes 2080 | tf_op jit(solution)/shard_map/ppermute | solution.py:14
  96.8 0.1 pad_maximum_fusion.1
  97.0 0.3 copy.131
  97.3 0.3 convolution_bitcast_fusion
  97.6 1.0 fusion.8
  98.6 4.5 %all-to-all-start.3 = ((f32[16,8,128]{2,1,0:T(8,128)}), f32[16,8,128]{2,1,0:T(8,128)S(1)}, u32[]{:S(2)}, u32[]{:S(2)}) async-start(f32[16,8,128]{2,1,0:T(8,128)} %fusion.8), calls=%async_computation.3 | async-start | bytes 131072 | tf_op jit(solution)/shard_map/all_to_all | solution.py:115
  103.1 0.8 copy.126
  103.9 9.7 %all-to-all-done.3 = f32[16,8,128]{2,1,0:T(8,128)S(1)} async-done(((f32[16,8,128]{2,1,0:T(8,128)}), f32[16,8,128]{2,1,0:T(8,128)S(1)}, u32[]{:S(2)}, u32[]{:S(2)}) %all-to-all-start.3) | async-done | bytes 65568 | tf_op jit(solution)/shard_map/all_to_all | solution.py:115
  113.6 3.5 %all-to-all-start.1 = ((bf16[16,128,4,1,16]{1,4,2,3,0:T(8,128)(2,1)}), bf16[16,128,4,1,16]{1,4,2,3,0:T(8,128)(2,1)S(1)}, u32[]{:S(2)}, u32[]{:S(2)}) async-start(bf16[16,128,4,1,16]{1,4,2,3,0:T(8,128)(2,1)} %copy.126), calls=%async_computation.1 | async-start | bytes 524288 | tf_op jit(solution)/shard_map/all_to_all | solution.py:101
  117.2 0.6 dynamic-slice.4
  118.5 6.0 %all-reduce = bf16[8,128]{1,0:T(8,128)(2,1)S(1)} all-reduce(f32[8,128]{1,0:T(8,128)S(1)} %reduce_sum.29), channel_id=2, replica_groups=mesh['u'=4,'v'=16,'tp'=4] {'tp'}, use_global_device_ids=true, to_apply=%region_3.4.clone | all-reduce | flops 1024 | bytes 6144
  124.5 0.5 dynamic-slice_convert_fusion
  125.0 4.7 %all-to-all-done.1 = bf16[16,128,4,1,16]{1,4,2,3,0:T(8,128)(2,1)S(1)} async-done(((bf16[16,128,4,1,16]{1,4,2,3,0:T(8,128)(2,1)}), bf16[16,128,4,1,16]{1,4,2,3,0:T(8,128)(2,1)S(1)}, u32[]{:S(2)}, u32[]{:S(2)}) %all-to-all-start.1) | async-done | bytes 262176 | tf_op jit(solution)/shard_map/all_to_all | solution.py:101
  129.8 0.9 copy.134
  (31 shorter events, 0.5 us)
Async XLA Ops:
  0.6 40.3 %copy-start.1 = (bf16[32,16,128]{2,1,0:T(8,128)(2,1)S(1)}, bf16[32,16,128]{2,1,0:T(8,128)(2,1)}, u32[]{:S(2)}) copy-start(bf16[32,16,128]{2,1,0:T(8,128)(2,1)} %param.15) | copy-start | bytes 393220
  5.3 35.6 %all-to-all-start = ((bf16[1,3,128,4,16,16]{2,5,3,1,0,4:T(8,128)(2,1)}), bf16[1,3,128,4,16,16]{2,5,3,1,0,4:T(8,128)(2,1)S(1)}, u32[]{:S(2)}, u32[]{:S(2)}) async-start(bf16[1,3,128,4,16,16]{2,5,3,1,0,4:T(8,128)(2,1)} %copy.109), calls=%async_computation | async-start | bytes 1572864 | tf_op jit(solution)/shard_map/all_to_all | solution.py:73
  41.8 51.3 %all-to-all-start.2 = ((bf16[4,32,16,128]{3,2,1,0:T(8,128)(2,1)}), bf16[4,32,16,128]{3,2,1,0:T(8,128)(2,1)S(1)}, u32[]{:S(2)}, u32[]{:S(2)}) async-start(bf16[4,32,16,128]{3,2,1,0:T(8,128)(2,1)} %broadcast_in_dim.12), calls=%async_computation.2 | async-start | bytes 1048576 | tf_op jit(solution)/shard_map/all_to_all | solution.py:77
  46.9 6.0 %collective-permute-start = (bf16[3,2,64]{1,2,0:T(8,128)(2,1)S(1)}, bf16[3,2,64]{1,2,0:T(8,128)(2,1)S(1)}, u32[]{:S(2)}, u32[]{:S(2)}) collective-permute-start(bf16[3,2,64]{1,2,0:T(8,128)(2,1)S(1)} %slice.161), channel_id=1, source_target_pairs={{0,64},{64,128},{128,192},{1,65},{65,129},{129,193},{2,66},{66,130... | collective-permute-start | bytes 2312 | tf_op jit(solution)/shard_map/ppermute | solution.py:14
  58.3 3.2 %copy-start = (f32[16,16,128,64]{2,3,1,0:T(8,128)}, f32[16,16,128,64]{2,3,1,0:T(8,128)S(1)}, u32[]{:S(2)}) copy-start(f32[16,16,128,64]{2,3,1,0:T(8,128)S(1)} %fusion.4) | copy-start | bytes 25165828
  67.0 12.5 %copy-start.2 = (f32[1024]{0:T(1024)S(1)}, f32[1024]{0:T(1024)}, u32[]{:S(2)}) copy-start(f32[1024]{0:T(1024)} %param.14) | copy-start | bytes 12292
  73.8 5.9 %collective-permute-start.3 = (f32[16,64]{1,0:T(8,128)S(1)}, f32[16,64]{1,0:T(8,128)S(1)}, u32[]{:S(2)}, u32[]{:S(2)}) collective-permute-start(f32[16,64]{1,0:T(8,128)S(1)} %fusion.25), channel_id=1, source_target_pairs={{0,192},{1,193},{2,194},{3,195},{4,196},{5,197},{6,198},{7,199},{8... | collective-permute-start | bytes 12296 | tf_op jit(solution)/shard_map/ppermute | solution.py:14
  74.4 5.5 %collective-permute-start.1 = (f32[16,64]{1,0:T(8,128)S(1)}, f32[16,64]{1,0:T(8,128)S(1)}, u32[]{:S(2)}, u32[]{:S(2)}) collective-permute-start(f32[16,64]{1,0:T(8,128)S(1)} %fusion.25), channel_id=1, source_target_pairs={{0,64},{64,128},{128,192},{1,65},{65,129},{129,193},{2,66},{66,130... | collective-permute-start | bytes 12296 | tf_op jit(solution)/shard_map/ppermute | solution.py:14
  78.2 7.0 %collective-permute-start.2 = (f32[16,64]{1,0:T(8,128)S(1)}, f32[16,64]{1,0:T(8,128)S(1)}, u32[]{:S(2)}, u32[]{:S(2)}) collective-permute-start(f32[16,64]{1,0:T(8,128)S(1)} %fusion.25), channel_id=1, source_target_pairs={{0,128},{64,192},{1,129},{65,193},{2,130},{66,194},{3,131},{67,195... | collective-permute-start | bytes 12296 | tf_op jit(solution)/shard_map/ppermute | solution.py:14
  85.3 31.9 %copy-start.3 = (u32[256]{0:T(256)S(1)}, u32[256]{0:T(256)}, u32[]{:S(2)}) copy-start(u32[256]{0:T(256)} %constant.46) | copy-start | bytes 3076
  91.2 5.6 %collective-permute-start.4 = (bf16[16,64]{0,1:T(8,128)(2,1)S(1)}, bf16[16,64]{0,1:T(8,128)(2,1)S(1)}, u32[]{:S(2)}, u32[]{:S(2)}) collective-permute-start(bf16[16,64]{0,1:T(8,128)(2,1)S(1)} %slice.189), channel_id=1, source_target_pairs={{64,0},{128,64},{192,128},{65,1},{129,65},{193,129},{66,2},{130,66... | collective-permute-start | bytes 6152 | tf_op jit(solution)/shard_map/ppermute | solution.py:14
  98.6 15.1 %all-to-all-start.3 = ((f32[16,8,128]{2,1,0:T(8,128)}), f32[16,8,128]{2,1,0:T(8,128)S(1)}, u32[]{:S(2)}, u32[]{:S(2)}) async-start(f32[16,8,128]{2,1,0:T(8,128)} %fusion.8), calls=%async_computation.3 | async-start | bytes 131072 | tf_op jit(solution)/shard_map/all_to_all | solution.py:115
  113.6 16.1 %all-to-all-start.1 = ((bf16[16,128,4,1,16]{1,4,2,3,0:T(8,128)(2,1)}), bf16[16,128,4,1,16]{1,4,2,3,0:T(8,128)(2,1)S(1)}, u32[]{:S(2)}, u32[]{:S(2)}) async-start(bf16[16,128,4,1,16]{1,4,2,3,0:T(8,128)(2,1)} %copy.126), calls=%async_computation.1 | async-start | bytes 524288 | tf_op jit(solution)/shard_map/all_to_all | solution.py:101
where the time goes:
time: 131 us
  waiting for transfers between devices  45.7 us (35%)
  starting transfers between devices  34.7 us (26%)
  local copies, waits for them, and re-layouts  27.7 us (21%)
  other arithmetic  9.19 us (7%)
  blocking collectives  6 us (5%)
  matrix products  5.52 us (4%)
  between operations  1.74 us (1%)
    all_to_all x1, waiting for transfers between devices, shards(): lax.all_to_all(stacked, 'v', split_axis=4, concat_axis=0, tiled=True)  20.5 us
    all_to_all x1, starting transfers between devices, shards(): lax.all_to_all(stacked, 'v', split_axis=4, concat_axis=0, tiled=True)  11 us
    ppermute x5, starting transfers between devices, from_behind(): return lax.ppermute(block, axis, route)  10.8 us
    ppermute x5, waiting for transfers between devices, from_behind(): return lax.ppermute(block, axis, route)  10.7 us
    all_to_all x1, waiting for transfers between devices, shards(): lax.all_to_all(partial_sum, 'v', split_axis=0, concat_axis=0, tiled=True)  9.73 us
    unnamed x17, local copies, waits for them, and re-layouts  8.32 us
    unnamed x1, blocking collectives  6 us
    slice x1, local copies, waits for them, and re-layouts, modal_conv(): ends = jnp.exp(-decays * (CHUNK - 1))[:, None, :] * running[:, :, -1, :]  5.46 us
  transfers between devices with their start and end apart: 9, of which 7 were waited for; matrix products, arithmetic and copies ran while one was open for 24% of the time, Pallas kernels for 0%

commit v1 on v0

--- a/solution.py
+++ b/solution.py
@@ -98,7 +98,9 @@
     carried = (convolved + gain * gated.astype(jnp.float32)).astype(jnp.bfloat16)
     op_cols = (query_short * carried.astype(jnp.float32)).astype(jnp.bfloat16)
     back = op_cols.reshape(width_v, tokens, width_u, 1, piece)
-    back = lax.all_to_all(back, "v", split_axis=0, concat_axis=3, tiled=True)
+    back = jnp.concatenate(
+        lax.all_to_all(jnp.stack(jnp.split(back, lax.axis_size("v"), axis=0)), "v", 0, 0), axis=3
+    )
     operator_out = back.reshape(tokens, chan_width)
     rim_rows = from_behind(op_cols[:STRIDE], "u", -1)
     extended = jnp.concatenate([op_cols, rim_rows], axis=0)

time: 131 us -> 137 us (1.046)
  local copies, waits for them, and re-layouts: 27.7 us -> 37.3 us
  waiting for transfers between devices: 45.7 us -> 41.1 us
    unnamed x17 -> x29, local copies, waits for them, and re-layouts: 8.32 us -> 17.4 us
    ppermute x5, waiting for transfers between devices: 10.7 us -> 7.51 us  [from_behind(): return lax.ppermute(block, axis, route)]
  transfers between devices with their start and end apart: 9 -> 9, of which waited for: 7 -> 6; matrix products, arithmetic and copies ran while one was open for 24% -> 25% of each run, Pallas kernels for 0% -> 0%
where the time goes in v1:
time: 137 us; the launch traced here: 136 us
  waiting for transfers between devices  41.1 us (30%)
  local copies, waits for them, and re-layouts  37.3 us (27%)
  starting transfers between devices  34.7 us (25%)
  other arithmetic  9.19 us (7%)
  blocking collectives  6.1 us (4%)
  matrix products  5.52 us (4%)
  between operations  1.76 us (1%)
    all_to_all x1, waiting for transfers between devices, shards(): lax.all_to_all(stacked, 'v', split_axis=4, concat_axis=0, tiled=True)  19.6 us
    unnamed x29, local copies, waits for them, and re-layouts  17.4 us
    all_to_all x1, starting transfers between devices, shards(): lax.all_to_all(stacked, 'v', split_axis=4, concat_axis=0, tiled=True)  11 us
    ppermute x5, starting transfers between devices, from_behind(): return lax.ppermute(block, axis, route)  10.8 us
    all_to_all x1, waiting for transfers between devices, shards(): lax.all_to_all(partial_sum, 'v', split_axis=0, concat_axis=0, tiled=True)  9.33 us
    ppermute x5, waiting for transfers between devices, from_behind(): return lax.ppermute(block, axis, route)  7.51 us
    unnamed x1, blocking collectives  6.1 us
    slice x1, local copies, waits for them, and re-layouts, modal_conv(): ends = jnp.exp(-decays * (CHUNK - 1))[:, None, :] * running[:, :, -1, :]  5.46 us
  transfers between devices with their start and end apart: 9, of which 6 were waited for; matrix products, arithmetic and copies ran while one was open for 25% of the time, Pallas kernels for 0%

profile of v1, /device:TPU:16, one launch (start us, length us, event | category | flops | bytes accessed | tf_op | source)
XLA Modules:
  0.0 135.7 jit_solution(4199759706810612827)
XLA Ops:
  0.6 1.2 copy.109
  1.8 1.1 copy.108
  2.9 1.1 copy.107
  4.2 1.1 copy.110
  5.3 11.0 %all-to-all-start = ((bf16[1,3,128,4,16,16]{2,5,3,1,0,4:T(8,128)(2,1)}), bf16[1,3,128,4,16,16]{2,5,3,1,0,4:T(8,128)(2,1)S(1)}, u32[]{:S(2)}, u32[]{:S(2)}) async-start(bf16[1,3,128,4,16,16]{2,5,3,1,0,4:T(8,128)(2,1)} %copy.110), calls=%async_computation | async-start | bytes 1572864 | tf_op jit(solution)/shard_map/all_to_all | solution.py:73
  16.3 0.9 reshape.238
  17.5 0.8 reshape_broadcast_in_dim.3
  18.3 1.0 reshape.244
  19.4 1.0 reshape.242
  20.9 0.2 multiply_exponential_fusion.1
  21.1 0.2 multiply_exponential_fusion.2
  21.3 19.6 %all-to-all-done = bf16[1,3,128,4,16,16]{2,5,3,1,0,4:T(8,128)(2,1)S(1)} async-done(((bf16[1,3,128,4,16,16]{2,5,3,1,0,4:T(8,128)(2,1)}), bf16[1,3,128,4,16,16]{2,5,3,1,0,4:T(8,128)(2,1)S(1)}, u32[]{:S(2)}, u32[]{:S(2)}) %all-to-all-start) | async-done | bytes 786464 | tf_op jit(solution)/shard_map/all_to_all | solution.py:73
  40.9 0.9 broadcast_in_dim.12
  41.8 4.8 %all-to-all-start.2 = ((bf16[4,32,16,128]{3,2,1,0:T(8,128)(2,1)}), bf16[4,32,16,128]{3,2,1,0:T(8,128)(2,1)S(1)}, u32[]{:S(2)}, u32[]{:S(2)}) async-start(bf16[4,32,16,128]{3,2,1,0:T(8,128)(2,1)} %broadcast_in_dim.12), calls=%async_computation.2 | async-start | bytes 1048576 | tf_op jit(solution)/shard_map/all_to_all | solution.py:77
  46.6 0.2 copy.160
  46.9 3.3 %collective-permute-start = (bf16[3,2,64]{1,2,0:T(8,128)(2,1)S(1)}, bf16[3,2,64]{1,2,0:T(8,128)(2,1)S(1)}, u32[]{:S(2)}, u32[]{:S(2)}) collective-permute-start(bf16[3,2,64]{1,2,0:T(8,128)(2,1)S(1)} %slice.177), channel_id=1, source_target_pairs={{0,64},{64,128},{128,192},{1,65},{65,129},{129,193},{2,66},{66,130... | collective-permute-start | bytes 2312 | tf_op jit(solution)/shard_map/ppermute | solution.py:14
  50.2 0.2 copy.113
  50.5 0.2 copy.118
  50.7 0.2 copy.121
  51.0 1.9 %collective-permute-done = bf16[3,2,64]{1,2,0:T(8,128)(2,1)S(1)} collective-permute-done((bf16[3,2,64]{1,2,0:T(8,128)(2,1)S(1)}, bf16[3,2,64]{1,2,0:T(8,128)(2,1)S(1)}, u32[]{:S(2)}, u32[]{:S(2)}) %collective-permute-start) | collective-permute-done | bytes 800 | tf_op jit(solution)/shard_map/ppermute | solution.py:14
  53.0 0.3 maximum_convert_fusion
  53.3 0.7 convert_bitcast_fusion
  54.0 4.2 %fusion.4 = f32[16,16,128,64]{2,3,1,0:T(8,128)S(1)} fusion(f32[16,128,64]{1,2,0:T(8,128)S(1)} %bitcast.129, f32[16,128,64]{1,2,0:T(8,128)S(1)} %multiply_exponential_fusion.1), kind=kOutput, calls=%fused_computation.5 | convolution fusion | flops 3223339008 | bytes 9437184 | tf_op jit(solution)/shard_map/ij,rkjc->rkic/dot_general | solution.py:37
  58.3 3.2 %copy-done = f32[16,16,128,64]{2,3,1,0:T(8,128)} copy-done((f32[16,16,128,64]{2,3,1,0:T(8,128)}, f32[16,16,128,64]{2,3,1,0:T(8,128)S(1)}, u32[]{:S(2)}) %copy-start) | copy-done | bytes 8388632
  61.5 5.5 %slice.201 = f32[16,16,1,64]{2,3,1,0:T(8,128)} slice(f32[16,16,128,64]{2,3,1,0:T(8,128)S(1)} %fusion.4), slice={[0:16], [0:16], [127:128], [0:64]} | slice | bytes 131072 | tf_op jit(solution)/shard_map/slice | solution.py:38
  67.0 5.4 %copy.139 = f32[16,16,1,64]{3,0,1,2:T(8,128)S(1)} copy(f32[16,16,1,64]{2,3,1,0:T(8,128)} %slice.201) | data formatting | bytes 131072 | tf_op jit(solution)/shard_map/squeeze | solution.py:38
  72.4 1.3 multiply_reduce_fusion.1
  73.8 0.7 collective-permute-start.3
  74.4 3.7 %collective-permute-start.1 = (f32[16,64]{1,0:T(8,128)S(1)}, f32[16,64]{1,0:T(8,128)S(1)}, u32[]{:S(2)}, u32[]{:S(2)}) collective-permute-start(f32[16,64]{1,0:T(8,128)S(1)} %fusion.25), channel_id=1, source_target_pairs={{0,64},{64,128},{128,192},{1,65},{65,129},{129,193},{2,66},{66,130... | collective-permute-start | bytes 12296 | tf_op jit(solution)/shard_map/ppermute | solution.py:14
  78.1 1.3 collective-permute-start.2
  79.6 0.4 collective-permute-done.1
  80.0 5.2 %collective-permute-done.2 = f32[16,64]{1,0:T(8,128)S(1)} collective-permute-done((f32[16,64]{1,0:T(8,128)S(1)}, f32[16,64]{1,0:T(8,128)S(1)}, u32[]{:S(2)}, u32[]{:S(2)}) %collective-permute-start.2) | collective-permute-done | bytes 4128 | tf_op jit(solution)/shard_map/ppermute | solution.py:14
  85.3 5.4 %multiply_reduce_fusion = f32[16,128,64]{1,2,0:T(8,128)S(1)} fusion(f32[16,16,128,64]{2,3,1,0:T(8,128)} %copy-done, f32[16,16,64]{2,1,0:T(8,128)S(1)} %multiply_add_fusion, f32[16,128,64]{1,2,0:T(8,128)S(1)} %get-tuple-element.42, f32[16,128,64]{1,2,0:T(8,128)S(1)} %get-tuple-element.41, f32[16,64]{1,0:T(8,128)S(1)} %get-tuple-element.38), kind=kLoop, calls=%fused_computation | loop fusion | flops 10354688 | bytes 10031104 | tf_op jit(solution)/shard_map/reduce_sum | solution.py:59
  90.7 0.4 fusion.19
  91.2 0.6 constant_dynamic-update-slice_fusion.15
  91.9 1.9 %collective-permute-start.4 = (bf16[16,64]{0,1:T(8,128)(2,1)S(1)}, bf16[16,64]{0,1:T(8,128)(2,1)S(1)}, u32[]{:S(2)}, u32[]{:S(2)}) collective-permute-start(bf16[16,64]{0,1:T(8,128)(2,1)S(1)} %slice.205), channel_id=1, source_target_pairs={{64,0},{128,64},{192,128},{65,1},{129,65},{193,129},{66,2},{130,66... | collective-permute-start | bytes 6152 | tf_op jit(solution)/shard_map/ppermute | solution.py:14
  93.8 0.6 constant_dynamic-update-slice_fusion.14
  94.4 0.6 constant_dynamic-update-slice_fusion.13
  95.0 0.6 constant_dynamic-update-slice_fusion.12
  95.6 0.6 constant_dynamic-update-slice_fusion.11
  96.2 0.6 constant_dynamic-update-slice_fusion.10
  96.8 0.6 constant_dynamic-update-slice_fusion.9
  97.4 0.6 constant_dynamic-update-slice_fusion.8
  98.0 0.6 constant_dynamic-update-slice_fusion.7
  98.6 0.6 constant_dynamic-update-slice_fusion.6
  99.2 0.6 constant_dynamic-update-slice_fusion.5
  99.8 0.6 constant_dynamic-update-slice_fusion.4
  100.5 0.6 constant_dynamic-update-slice_fusion.3
  101.1 0.6 constant_dynamic-update-slice_fusion.2
  101.7 0.3 copy.128
  102.0 0.1 pad_maximum_fusion.1
  102.1 0.3 copy.131
  102.4 0.3 convolution_bitcast_fusion
  102.7 1.0 fusion.8
  103.7 4.5 %all-to-all-start.3 = ((f32[16,8,128]{2,1,0:T(8,128)}), f32[16,8,128]{2,1,0:T(8,128)S(1)}, u32[]{:S(2)}, u32[]{:S(2)}) async-start(f32[16,8,128]{2,1,0:T(8,128)} %fusion.8), calls=%async_computation.3 | async-start | bytes 131072 | tf_op jit(solution)/shard_map/all_to_all | solution.py:117
  108.2 0.6 constant_dynamic-update-slice_fusion.1
  108.8 0.6 constant_dynamic-update-slice_fusion
  109.4 9.3 %all-to-all-done.3 = f32[16,8,128]{2,1,0:T(8,128)S(1)} async-done(((f32[16,8,128]{2,1,0:T(8,128)}), f32[16,8,128]{2,1,0:T(8,128)S(1)}, u32[]{:S(2)}, u32[]{:S(2)}) %all-to-all-start.3) | async-done | bytes 65568 | tf_op jit(solution)/shard_map/all_to_all | solution.py:117
  118.8 3.5 %all-to-all-start.1 = ((bf16[16,1,128,4,1,16]{2,5,4,3,1,0:T(8,128)(2,1)}), bf16[16,1,128,4,1,16]{2,5,4,3,1,0:T(8,128)(2,1)S(1)}, u32[]{:S(2)}, u32[]{:S(2)}) async-start(bf16[16,1,128,4,1,16]{2,5,4,3,1,0:T(8,128)(2,1)} %constant_dynamic-update-slice_fusion), calls=%async_computation.1 | async-start | bytes 524288 | tf_op jit(solution)/shard_map/all_to_all | solution.py:102
  122.3 0.6 dynamic-slice.4
  123.6 6.1 %all-reduce = bf16[8,128]{1,0:T(8,128)(2,1)S(1)} all-reduce(f32[8,128]{1,0:T(8,128)S(1)} %reduce_sum.29), channel_id=2, replica_groups=mesh['u'=4,'v'=16,'tp'=4] {'tp'}, use_global_device_ids=true, to_apply=%region_3.4.clone | all-reduce | flops 1024 | bytes 6144
  129.7 0.5 dynamic-slice_convert_fusion
  130.2 4.7 %all-to-all-done.1 = bf16[16,1,128,4,1,16]{2,5,4,3,1,0:T(8,128)(2,1)S(1)} async-done(((bf16[16,1,128,4,1,16]{2,5,4,3,1,0:T(8,128)(2,1)}), bf16[16,1,128,4,1,16]{2,5,4,3,1,0:T(8,128)(2,1)S(1)}, u32[]{:S(2)}, u32[]{:S(2)}) %all-to-all-start.1) | async-done | bytes 262176 | tf_op jit(solution)/shard_map/all_to_all | solution.py:102
  134.9 0.9 copy.134
  (44 shorter events, 1.7 us)
Async XLA Ops:
  0.6 40.3 %copy-start.1 = (bf16[32,16,128]{2,1,0:T(8,128)(2,1)S(1)}, bf16[32,16,128]{2,1,0:T(8,128)(2,1)}, u32[]{:S(2)}) copy-start(bf16[32,16,128]{2,1,0:T(8,128)(2,1)} %param.15) | copy-start | bytes 393220
  5.3 35.6 %all-to-all-start = ((bf16[1,3,128,4,16,16]{2,5,3,1,0,4:T(8,128)(2,1)}), bf16[1,3,128,4,16,16]{2,5,3,1,0,4:T(8,128)(2,1)S(1)}, u32[]{:S(2)}, u32[]{:S(2)}) async-start(bf16[1,3,128,4,16,16]{2,5,3,1,0,4:T(8,128)(2,1)} %copy.110), calls=%async_computation | async-start | bytes 1572864 | tf_op jit(solution)/shard_map/all_to_all | solution.py:73
  41.8 37.7 %all-to-all-start.2 = ((bf16[4,32,16,128]{3,2,1,0:T(8,128)(2,1)}), bf16[4,32,16,128]{3,2,1,0:T(8,128)(2,1)S(1)}, u32[]{:S(2)}, u32[]{:S(2)}) async-start(bf16[4,32,16,128]{3,2,1,0:T(8,128)(2,1)} %broadcast_in_dim.12), calls=%async_computation.2 | async-start | bytes 1048576 | tf_op jit(solution)/shard_map/all_to_all | solution.py:77
  46.9 6.0 %collective-permute-start = (bf16[3,2,64]{1,2,0:T(8,128)(2,1)S(1)}, bf16[3,2,64]{1,2,0:T(8,128)(2,1)S(1)}, u32[]{:S(2)}, u32[]{:S(2)}) collective-permute-start(bf16[3,2,64]{1,2,0:T(8,128)(2,1)S(1)} %slice.177), channel_id=1, source_target_pairs={{0,64},{64,128},{128,192},{1,65},{65,129},{129,193},{2,66},{66,130... | collective-permute-start | bytes 2312 | tf_op jit(solution)/shard_map/ppermute | solution.py:14
  58.3 3.2 %copy-start = (f32[16,16,128,64]{2,3,1,0:T(8,128)}, f32[16,16,128,64]{2,3,1,0:T(8,128)S(1)}, u32[]{:S(2)}) copy-start(f32[16,16,128,64]{2,3,1,0:T(8,128)S(1)} %fusion.4) | copy-start | bytes 25165828
  73.8 5.8 %collective-permute-start.3 = (f32[16,64]{1,0:T(8,128)S(1)}, f32[16,64]{1,0:T(8,128)S(1)}, u32[]{:S(2)}, u32[]{:S(2)}) collective-permute-start(f32[16,64]{1,0:T(8,128)S(1)} %fusion.25), channel_id=1, source_target_pairs={{0,192},{1,193},{2,194},{3,195},{4,196},{5,197},{6,198},{7,199},{8... | collective-permute-start | bytes 12296 | tf_op jit(solution)/shard_map/ppermute | solution.py:14
  74.4 5.5 %collective-permute-start.1 = (f32[16,64]{1,0:T(8,128)S(1)}, f32[16,64]{1,0:T(8,128)S(1)}, u32[]{:S(2)}, u32[]{:S(2)}) collective-permute-start(f32[16,64]{1,0:T(8,128)S(1)} %fusion.25), channel_id=1, source_target_pairs={{0,64},{64,128},{128,192},{1,65},{65,129},{129,193},{2,66},{66,130... | collective-permute-start | bytes 12296 | tf_op jit(solution)/shard_map/ppermute | solution.py:14
  78.1 7.0 %collective-permute-start.2 = (f32[16,64]{1,0:T(8,128)S(1)}, f32[16,64]{1,0:T(8,128)S(1)}, u32[]{:S(2)}, u32[]{:S(2)}) collective-permute-start(f32[16,64]{1,0:T(8,128)S(1)} %fusion.25), channel_id=1, source_target_pairs={{0,128},{64,192},{1,129},{65,193},{2,130},{66,194},{3,131},{67,195... | collective-permute-start | bytes 12296 | tf_op jit(solution)/shard_map/ppermute | solution.py:14
  85.3 37.0 %copy-start.2 = (u32[256]{0:T(256)S(1)}, u32[256]{0:T(256)}, u32[]{:S(2)}) copy-start(u32[256]{0:T(256)} %constant.46) | copy-start | bytes 3076
  91.9 10.1 %collective-permute-start.4 = (bf16[16,64]{0,1:T(8,128)(2,1)S(1)}, bf16[16,64]{0,1:T(8,128)(2,1)S(1)}, u32[]{:S(2)}, u32[]{:S(2)}) collective-permute-start(bf16[16,64]{0,1:T(8,128)(2,1)S(1)} %slice.205), channel_id=1, source_target_pairs={{64,0},{128,64},{192,128},{65,1},{129,65},{193,129},{66,2},{130,66... | collective-permute-start | bytes 6152 | tf_op jit(solution)/shard_map/ppermute | solution.py:14
  103.7 15.1 %all-to-all-start.3 = ((f32[16,8,128]{2,1,0:T(8,128)}), f32[16,8,128]{2,1,0:T(8,128)S(1)}, u32[]{:S(2)}, u32[]{:S(2)}) async-start(f32[16,8,128]{2,1,0:T(8,128)} %fusion.8), calls=%async_computation.3 | async-start | bytes 131072 | tf_op jit(solution)/shard_map/all_to_all | solution.py:117
  118.8 16.1 %all-to-all-start.1 = ((bf16[16,1,128,4,1,16]{2,5,4,3,1,0:T(8,128)(2,1)}), bf16[16,1,128,4,1,16]{2,5,4,3,1,0:T(8,128)(2,1)S(1)}, u32[]{:S(2)}, u32[]{:S(2)}) async-start(bf16[16,1,128,4,1,16]{2,5,4,3,1,0:T(8,128)(2,1)} %constant_dynamic-update-slice_fusion), calls=%async_computation.1 | async-start | bytes 524288 | tf_op jit(solution)/shard_map/all_to_all | solution.py:102
